TPU v7x, 32 devices: a whole 2x2x4 slice. The times are simulated.
32 devices in a mesh: gx: 4 (over z), gy: 8 (over y, x, core).
Axes of the slice: x: 2, y: 2, z: 4, core: 2. Of those that a mesh axis runs over, the one named last changes fastest.
Arguments:
- enthalpy: float32 [32, 256, 128], P('gx', 'gy'), may hold values from 0 to 2.5
- porosity: float32 [32, 256, 128], P('gx', 'gy'), may hold values from 0.05 to 0.85
- active: int32 [8, 16], P('gx', 'gy'), may hold values from 0 to 1, as said below
- move_count: int32 [4, 8, 2], P('gx', 'gy'), may hold values from 0 to 2, as said below
- move_slot: int32 [4, 8, 2, 2], P('gx', 'gy'), may hold values from 0 to 3, as said below
Outputs:
- enthalpy_out: float32 [4, 8, 4, 4, 16, 128], P('gx', 'gy')
- porosity_out: float32 [4, 8, 4, 4, 16, 128], P('gx', 'gy')
Inputs may be any that keep to these rules, and one draw needn't show every extreme that they name: Before balancing some devices hold several active tiles; after both rounds each device holds at most 2 active tiles, and some device holds exactly 2. `move_count`: A device and its partner in a round carry the same count; some pair in each round trades 2 tiles. `move_slot`: the 2 entries of a device and round are distinct slots; only the first move_count of them are used.
All inputs are finite; a program needn't handle non-finite values.
Results may differ from a plain program's by a relative error of at most 0.0003.
Values may be sent and summed in bfloat16 or wider, within the bound.
No kernel may reach another device: no remote copies, remote signals or barrier semaphores. Data moves between devices by JAX's collectives and lax.ppermute only.
A program may use at most 64 MiB of HBM per device.

v0:
```python
import jax
import jax.numpy as jnp
from jax import lax
from jax.experimental import pallas as pl
from jax.experimental.pallas import tpu as pltpu
from jax.sharding import PartitionSpec as P


PAIRS = 4
DEEP = 2 * PAIRS
EARLY = PAIRS // 2
SUB = 8
LANES = 128
VMEM_LIMIT = 16 * 2**20

HEAT_SCALE = 16000.0
HEAT_SHIFT = 20000.0
PORE_SCALE = 25000.0
PORE_SHIFT = 7750.0


def encode(values, scale, shift):
    codes = jnp.floor(values * scale + (0.5 - shift))
    return jnp.clip(codes, -32768.0, 32767.0).astype(jnp.int32).astype(jnp.int16)


def decode(codes, scale, shift):
    return (codes.astype(jnp.int32).astype(jnp.float32) + shift) * (1.0 / scale)


def flag_rows(active_ref, cols):
    lane = lax.broadcasted_iota(jnp.int32, (cols, LANES), 1)
    col = lax.broadcasted_iota(jnp.int32, (cols, LANES), 0)

    def flag(i):
        return jnp.where(col < cols // 2, active_ref[i, 0], active_ref[i, 1])

    return jnp.where(lane < LANES // 2, flag(0), flag(1)).astype(jnp.float32)


def mask_at(ranks):
    choose = lambda i, k, s: (i * ranks + k) * 4 + s
    taken = lambda i, r, s: 8 * ranks + (i * ranks + r) * 4 + s
    again = lambda k, r: 16 * ranks + k * ranks + r
    return choose, taken, again, 16 * ranks + ranks * ranks


def pack_x(
    active_ref, count_ref, slot_ref, heat_ref, pore_ref, out_ref, heat_out, pore_out, mask_ref
):
    rows, cols = heat_ref.shape[0], heat_ref.shape[1]
    ranks = slot_ref.shape[1]
    out_ref[0:rows] = heat_ref[...].astype(jnp.bfloat16)
    out_ref[rows : 2 * rows] = pore_ref[...].astype(jnp.bfloat16)
    out_ref[2 * rows] = flag_rows(active_ref, cols).astype(jnp.bfloat16)
    heat_out[...] = heat_ref[...]
    pore_out[...] = pore_ref[...]
    choose, taken, again, _ = mask_at(ranks)

    def put(row, holds):
        mask_ref[row] = jnp.full((SUB, LANES), jnp.where(holds, 1.0, 0.0), jnp.float32)

    for i in range(2):
        for k in range(ranks):
            for s in range(4):
                here = slot_ref[i, k] == s
                put(choose(i, k, s), here)
                put(taken(i, k, s), here & (k < count_ref[i]))
    for k in range(ranks):
        for r in range(ranks):
            put(again(k, r), (slot_ref[1, k] == slot_ref[0, r]) & (r < count_ref[0]))


def inside(axis, below):
    at = lax.axis_index(axis)
    has = at < lax.axis_size(axis) - 1 if below else at > 0
    return jnp.where(has, 1.0, 0.0).astype(jnp.float32)


def x_parts(own_ref, first_ref, second_ref):
    odd = lax.rem(lax.axis_index("gx") + lax.axis_index("gy"), 2)
    return ((2 - 2 * odd, first_ref), (1, own_ref), (2 * odd, second_ref))


def pack_y(own_ref, first_ref, second_ref, near_out, far_out):
    rows = (own_ref.shape[0] - 1) // 2
    cols = own_ref.shape[1]
    side = 2 * rows
    odd = lax.rem(lax.axis_index("gy"), 2)
    edge = cols - DEEP
    sub = lax.broadcasted_iota(jnp.int32, (DEEP, LANES), 0)
    sides = ((near_out, edge - edge * odd, odd == 0), (far_out, edge * odd, odd == 1))
    for out_ref, start, right in sides:
        at = pl.ds(pl.multiple_of(start, DEEP), DEEP)
        flags = jnp.zeros((DEEP, LANES), jnp.float32)
        for i, part in x_parts(own_ref, first_ref, second_ref):
            flags = jnp.where(sub == i, part[2 * rows, at, :].astype(jnp.float32), flags)
            for f in range(2):
                if part is own_ref:
                    out_ref[pl.ds(f * side, rows)] = part[pl.ds(f * rows, rows), at, :]
                    continue
                for d in range(1, rows // 2 + 1):
                    a, b = (
                        part[f * rows + jnp.where(i == 0, rows - e, e - 1), at, :].astype(jnp.float32)
                        for e in (d, rows - d)
                    )
                    if d < rows - d:
                        a = jnp.where(
                            right,
                            jnp.where(sub >= d, a, pltpu.roll(b, d, 0)),
                            jnp.where(sub < DEEP - d, a, pltpu.roll(b, DEEP - d, 0)),
                        )
                    out_ref[f * side + rows + (i // 2) * (rows // 2) + d - 1] = a.astype(jnp.bfloat16)
        out_ref[2 * side] = flags.astype(jnp.bfloat16)


def edge_row(part, field, x, rows, right):
    side = 2 * rows
    if rows <= x < 2 * rows:
        return part[field * side + x - rows].astype(jnp.float32)
    d = rows - x if x < rows else x - 2 * rows + 1
    at = field * side + rows + (0 if x < rows else rows // 2) - 1
    if d <= rows // 2:
        return part[at + d].astype(jnp.float32)
    if d == rows:
        return part[at + rows // 2].astype(jnp.float32)
    v = part[at + rows - d].astype(jnp.float32)
    return jnp.where(right, pltpu.roll(v, d, 0), pltpu.roll(v, DEEP - d, 0))


def flux_sums(parts, twice):
    lane = lax.broadcasted_iota(jnp.int32, (SUB, LANES), 1)
    depths = []
    for val, wgt, lo, hi in parts:
        depths.append(
            {
                (c, j): [
                    (pltpu.roll(v, by, 1), pltpu.roll(w, by, 1))
                    for by in ((LANES - 1,) if twice else (LANES - 1, 1))
                ]
                for c in range(lo, hi)
                for j, (v, w) in enumerate(zip(val[c], wgt[c]))
            }
        )
    for (val, wgt, _, _), depth in zip(parts, depths):
        for (c, j), shifted in depth.items():
            f = None
            for (v, w), ok in zip(shifted, (lane < LANES - 1, lane > 0)):
                g = jnp.where(ok, (wgt[c][j] + w) * (v - val[c][j]), 0.0)
                f = g if f is None else f + g
            depth[c, j] = f
    for depth in depths:
        for at, f in depth.items():
            depth[at] = f - pltpu.roll(f, 1, 1) if twice else f

    sums = []
    for (val, wgt, lo, hi), depth in zip(parts, depths):
        n = len(val[lo])
        span = range(n)

        def toward(c):
            return [(wgt[c][j] + wgt[c + 1][j]) * (val[c + 1][j] - val[c][j]) for j in span]

        out = {}
        last = toward(lo - 1)
        for c in range(lo, hi):
            v, w = val[c], wgt[c]
            ahead = toward(c)
            down = [(w[j] + w[j + 1]) * (v[j + 1] - v[j]) for j in range(n - 1)]
            down.append(
                (w[n - 1] + pltpu.roll(w[0], SUB - 1, 0))
                * (pltpu.roll(v[0], SUB - 1, 0) - v[n - 1])
            )
            up = [pltpu.roll(down[-1], 1, 0)] + down[:-1]
            out[c] = [(ahead[j] - last[j]) + (down[j] - up[j]) + depth[c, j] for j in span]
            last = ahead
        sums.append(out)
    return sums


def advance(*parts, twice=True):
    fluxes = []
    for pore, h, q, lo, hi, _ in parts:
        val, wgt = {}, {}
        for c in range(lo - 1, hi + 1):
            t = [jnp.tanh(v) for v in h[c]]
            temp = [2.5 * v - u for v, u in zip(h[c], t)]
            if pore:
                val[c] = q[c]
                wgt[c] = [1.0 + jnp.tanh(v) for v in temp]
            else:
                val[c] = temp
                wgt[c] = [(1.0 - v) * (1.0 - v) * (u + 7.0 / 3.0) for v, u in zip(q[c], t)]
        fluxes.append((val, wgt, lo, hi))
    results = []
    for (pore, h, q, lo, hi, mask), (val, wgt, _, _), acc in zip(parts, fluxes, flux_sums(fluxes, twice)):
        new = {}
        for c in range(lo, hi):
            if pore:
                new[c] = [
                    v + m * (a - 4.0 * r * v)
                    for v, m, a, r in zip(q[c], mask(c, 1), acc[c], wgt[c])
                ]
            else:
                new[c] = [v + m * a for v, m, a in zip(h[c], mask(c, 0), acc[c])]
        results.append(new)
    return results


def tile_rows(marks, i, tx, n, out):
    low = lax.broadcasted_iota(jnp.int32, (SUB, LANES), 1) < LANES // 2
    sub = lax.broadcasted_iota(jnp.int32, (SUB, LANES), 0)
    other = pltpu.roll(marks, LANES // 2, 1)
    for h, flag in ((0, jnp.where(low, marks, other)), (1, jnp.where(low, other, marks))):
        first = (2 * i + h) * tx
        for j in range(n):
            x = sub * n + j
            out[j] = jnp.where((x >= first) & (x < first + tx), flag, out[j])
    return out


def scalings(flags):
    return ([0.009 * f for f in flags], [0.0375 * f for f in flags])


def back(columns, wide, turn, rows, total, heat):
    for c, column in enumerate(columns):
        n = len(column)
        for j, v in enumerate(column):
            wide[pl.ds(c * total + j, SUB, stride=n), :] = 0.5 * v + 1.0 if heat else v
    for c in range(len(columns)):
        turn[pl.ds(c * rows, rows), :] = wide[pl.ds(c * total + DEEP, rows), :]


def inner(
    own_ref, heat_ref, pore_ref, xa_ref, xb_ref,
    heat_out, pore_out, heat_save, pore_save, flag_out, wide,
):
    rows, cols = heat_ref.shape[0], heat_ref.shape[1]
    total = rows + 2 * DEEP
    width = cols + 2 * DEEP
    n = total // SUB
    tx, ty = rows // 2, cols // 2
    f32 = jnp.float32
    odd = lax.rem(lax.axis_index("gx") + lax.axis_index("gy"), 2)

    def row(i, r):
        if i == 1:
            return own_ref[r].astype(f32)
        pair = (xa_ref[r], xb_ref[r]) if i == 0 else (xb_ref[r], xa_ref[r])
        v = jnp.where(odd == 1, *pair).astype(f32)
        return v * inside("gx", i == 2)

    flags = []
    marks = [row(i, 2 * rows) for i in range(3)]
    for k in range(2):
        f = [jnp.zeros((SUB, LANES), f32) for _ in range(n)]
        for i in range(3):
            f = tile_rows(marks[i][k * ty : k * ty + SUB], i, tx, n, f)
        for j in range(n):
            flag_out[k, j] = f[j]
        flags.append(scalings(f))

    def mask(c, kind):
        return flags[0 if c < DEEP + ty else 1][kind]

    h, q = {}, {}
    for field, home, state in ((0, heat_ref, h), (1, pore_ref, q)):
        for i in range(3):
            for r in range(rows):
                v = home[r] if i == 1 else row(i, field * rows + r)
                v = 2.0 * v - 2.0 if field == 0 else v
                for g in range(0, cols, SUB):
                    at = g * total + (i * rows + r) * SUB
                    wide[field, at : at + SUB, :] = v[g : g + SUB]
        for c in range(cols):
            at = c // SUB * SUB * total + c % SUB
            state[DEEP + c] = [
                wide[field, pl.ds(at + j * SUB, SUB, stride=n * SUB), :] for j in range(n)
            ]

    for p in range(EARLY):
        lo, hi = DEEP + 2 * p + 1, width - DEEP - 2 * p - 1
        for side, c in ((0, lo), (1, hi - 1)):
            for j in range(n):
                heat_save[p, side, j] = h[c][j]
        h.update(*advance((False, h, q, lo, hi, mask)))
        lo, hi = lo + 1, hi - 1
        for side, c in ((0, lo), (1, hi - 1)):
            for j in range(n):
                pore_save[p, side, j] = q[c][j]
        q.update(*advance((True, h, q, lo, hi, mask)))
    for state, out in ((h, heat_out), (q, pore_out)):
        for c in range(cols):
            for j in range(n):
                out[c, j] = state[DEEP + c][j]


def halo(near, flag_ref, got_ref, wide, rows, n):
    total = n * SUB
    tx = rows // 2
    f32 = jnp.float32
    odd = lax.rem(lax.axis_index("gy"), 2)
    side = 1 - odd if near else odd
    left = side == 0
    has = None if near else jnp.where(left, inside("gy", False), inside("gy", True))
    row_open = (inside("gx", False), None, inside("gx", True))

    def scaled(v, *by):
        for s in by:
            v = v if s is None else v * s
        return v

    marks = scaled(got_ref[4 * rows].astype(f32), has)
    beyond = [jnp.zeros((SUB, LANES), f32) for _ in range(n)]
    for i in range(3):
        row = jnp.broadcast_to(scaled(marks[i : i + 1], row_open[i]), (SUB, LANES))
        beyond = tile_rows(row, i, tx, n, beyond)
    flags = [scalings(beyond), scalings([flag_ref[side, j] for j in range(n)])]

    def mask(c, kind):
        return flags[0 if c < DEEP else 1][kind]

    states = ({}, {})
    for field, state in enumerate(states):
        for x in range(total):
            v = scaled(edge_row(got_ref, field, x, rows, left), has, row_open[x // rows])
            wide[field, x * DEEP : (x + 1) * DEEP, :] = 2.0 * v - 2.0 if field == 0 else v
        for c in range(DEEP):
            state[c] = [
                jnp.where(
                    left,
                    wide[field, pl.ds(j * DEEP + c, SUB, stride=n * DEEP), :],
                    wide[field, pl.ds(j * DEEP + DEEP - 1 - c, SUB, stride=n * DEEP), :],
                )
                for j in range(n)
            ]
    return side, left, states, mask


def strips(h, q, left, wide, turn, rows, n):
    total = n * SUB
    for field, state in ((0, h), (1, q)):
        for c in range(DEEP):
            for j, v in enumerate(state[DEEP + c]):
                wide[field, pl.ds(c * total + j, SUB, stride=n), :] = (
                    0.5 * v + 1.0 if field == 0 else v
                )
        for c in range(DEEP):
            at = pl.multiple_of(jnp.where(left, c, DEEP - 1 - c) * rows, SUB)
            turn[field, pl.ds(at, rows), :] = wide[field, pl.ds(c * total + DEEP, rows), :]


def middle(
    heat_in, pore_in, heat_save, pore_save, flag_ref, got_ref,
    heat_strip, pore_strip, heat_mid, pore_mid, heat_edge, pore_edge, heat_kept, pore_kept,
    wide, turn, wide_mid, turn_mid,
):
    rows, cols = heat_mid.shape[0], heat_in.shape[0]
    n = heat_in.shape[1]
    width = cols + 2 * DEEP
    total = n * SUB
    ty = cols // 2
    span = range(n)
    side, left, (hw, qw), mask_w = halo(True, flag_ref, got_ref, wide, rows, n)
    flags = [scalings([flag_ref[k, j] for j in span]) for k in range(2)]

    def mask(c, kind):
        return flags[0 if c < DEEP + ty else 1][kind]

    h = {DEEP + c: [heat_in[c, j] for j in span] for c in range(cols)}
    q = {DEEP + c: [pore_in[c, j] for j in span] for c in range(cols)}

    def pick(low, high):
        return [jnp.where(left, a, b) for a, b in zip(low, high)]

    def at(state, c):
        return pick(state[c], state[width - 1 - c])

    kept = ({}, {})
    for p in range(EARLY):
        for keep, save, out in zip(kept, (heat_save, pore_save), (heat_kept, pore_kept)):
            keep[p] = [save[p, side, j] for j in span]
            for j in span:
                out[p, j] = save[p, 1 - side, j]

    def keep_now(field, state, p, c):
        low, high = state[c], state[width - 1 - c]
        kept[field][p] = pick(low, high)
        for j, v in enumerate(pick(high, low)):
            (heat_kept, pore_kept)[field][p, j] = v

    waiting = []

    def block_half(step):
        p, k = EARLY + step // 4, step % 4
        pore = k >= 2
        lo = DEEP + 2 * p + (2 if pore else 1)
        if k % 2 == 0:
            keep_now(int(pore), q if pore else h, p, lo)
        half = (lo, width // 2) if k % 2 == 0 else (width // 2, width - lo)
        return (pore, h, q, *half, mask)

    for p in range(PAIRS):
        for pore in (False, True):
            step = 2 * p + pore
            lo = 2 * p + 1 + pore
            end = block_half(step)
            if pore:
                hw[lo + DEEP - 1], hw[lo + DEEP] = at(h, lo + DEEP - 1), at(h, lo + DEEP)
                then = dict(qw)
                then[lo + DEEP] = kept[1][p]
                part = (True, hw, then, lo, lo + DEEP, mask_w)
            else:
                c = lo + DEEP - 1
                hw[c] = at(h, c)
                qw[c], qw[c + 1] = at(q, c), at(q, c + 1)
                then = dict(hw)
                then[c + 1] = kept[0][p]
                part = (False, then, qw, lo, lo + DEEP, mask_w)
            new, ours = advance(part, end)
            (qw if pore else hw).update(new)
            waiting.append(ours)
            if step % 2 == 1:
                for result in waiting:
                    (q if end[0] else h).update(result)
                waiting = []

    strips(hw, qw, left, wide, turn, rows, n)
    for field, out in ((0, heat_strip), (1, pore_strip)):
        for r in range(rows):
            out[r] = turn[field, pl.ds(r, DEEP, stride=rows), :]
    for field, state, edge, mid in ((0, h, heat_edge, heat_mid), (1, q, pore_edge, pore_mid)):
        for c in range(DEEP + 1):
            for j, v in enumerate(pick(state[width - 1 - DEEP - c], state[DEEP + c])):
                edge[c, j] = v
        back(
            [state[c] for c in range(2 * DEEP, width - 2 * DEEP)], wide_mid.at[field],
            turn_mid.at[field], rows, total, field == 0,
        )
        for r in range(rows):
            for g in range(0, cols - 2 * DEEP, SUB):
                mid[r, g : g + SUB] = turn_mid[field, pl.ds(g * rows + r, SUB, stride=rows), :]


def far_edge(
    mask_ref, heat_edge, pore_edge, heat_kept, pore_kept, heat_mid, pore_mid, flag_ref, got_ref,
    heat_near, pore_near, block, send_ref, wide, turn,
):
    rows, cols = heat_mid.shape[0], heat_mid.shape[1] + 2 * DEEP
    n = heat_edge.shape[1]
    span = range(n)
    side, left, (h, q), mask = halo(False, flag_ref, got_ref, wide, rows, n)
    for state, edge in ((h, heat_edge), (q, pore_edge)):
        for c in range(DEEP + 1):
            state[DEEP + c] = [edge[c, j] for j in span]
    for p in range(PAIRS):
        lo = 2 * p + 1
        then = dict(h)
        then[lo + DEEP] = [heat_kept[p, j] for j in span]
        h.update(*advance((False, then, q, lo, lo + DEEP, mask), twice=False))
        lo = lo + 1
        then = dict(q)
        then[lo + DEEP] = [pore_kept[p, j] for j in span]
        q.update(*advance((True, h, then, lo, lo + DEEP, mask), twice=False))
    strips(h, q, left, wide, turn, rows, n)
    end = cols - DEEP
    far_at = pl.ds(pl.multiple_of(end * side, SUB), DEEP)
    near_at = pl.ds(pl.multiple_of(end - end * side, SUB), DEEP)
    for field, mid, near in ((0, heat_mid, heat_near), (1, pore_mid, pore_near)):
        for r in range(rows):
            block[field, r, DEEP:end] = mid[r]
            block[field, r, near_at] = near[r]
            block[field, r, far_at] = turn[field, pl.ds(r, DEEP, stride=rows), :]
    chosen(mask_ref, 0, block, send_ref)


def tile_of(block, field, s):
    tx, ty = block.shape[1] // 2, block.shape[2] // 2
    i, k = s // 2, s % 2
    return block[field, i * tx : (i + 1) * tx, k * ty : (k + 1) * ty, :]


def chosen(mask_ref, i, block, out):
    choose = mask_at(out.shape[0])[0]
    for field, scale, shift in ((0, HEAT_SCALE, HEAT_SHIFT), (1, PORE_SCALE, PORE_SHIFT)):
        for k in range(out.shape[0]):
            v = tile_of(block, field, 0)
            for s in range(1, 4):
                v = jnp.where(
                    held(mask_ref, choose(i, k, s), v.shape), tile_of(block, field, s), v
                )
            out[k, field] = encode(v, scale, shift)


def split(mask_ref, block, heat_out, pore_out, later_ref):
    for field, out in ((0, heat_out), (1, pore_out)):
        for s in range(4):
            out[s] = tile_of(block, field, s)
    chosen(mask_ref, 1, block, later_ref)


def held(mask_ref, row, shape):
    m = mask_ref[row]
    m = jnp.concatenate([m] * (shape[1] // SUB), axis=0)
    return jnp.broadcast_to(m[None], shape) > 0.5


def resend(mask_ref, got_ref, local_ref, send_ref):
    ranks = got_ref.shape[0]
    shape = got_ref.shape[2:]
    again = mask_at(ranks)[2]
    for k in range(ranks):
        for f in range(2):
            v = local_ref[k, f].astype(jnp.int32)
            for r in range(ranks):
                v = jnp.where(
                    held(mask_ref, again(k, r), shape), got_ref[r, f].astype(jnp.int32), v
                )
            send_ref[k, f] = v.astype(jnp.int16)


def place(mask_ref, heat_ref, pore_ref, first_ref, second_ref, heat_out, pore_out):
    ranks = first_ref.shape[0]
    shape = first_ref.shape[2:]
    taken = mask_at(ranks)[1]
    for field, src, out, scale, shift in (
        (0, heat_ref, heat_out, HEAT_SCALE, HEAT_SHIFT),
        (1, pore_ref, pore_out, PORE_SCALE, PORE_SHIFT),
    ):
        came = [
            (i, r, decode(got[r, field], scale, shift))
            for i, got in ((0, first_ref), (1, second_ref))
            for r in range(ranks)
        ]
        for s in range(4):
            v = src[s]
            for i, r, tile in came:
                v = jnp.where(held(mask_ref, taken(i, r, s), shape), tile, v)
            out[s] = v


def call(body, spec, outs, scratch=(), out_space=pltpu.VMEM):
    def run(*args):
        space = {"s": pltpu.SMEM, "v": pltpu.VMEM, "V": pltpu.VMEM}
        args = [
            pltpu.with_memory_space_constraint(a, pltpu.VMEM if c == "V" else pltpu.HBM)
            for c, a in zip(spec, args)
        ]
        shapes = [
            pltpu.VMEM(s, d) if out_space is not None else jax.ShapeDtypeStruct(s, d)
            for s, d in outs
        ]
        return pl.pallas_call(
            body,
            in_specs=[pl.BlockSpec(memory_space=space[c]) for c in spec],
            out_specs=[pl.BlockSpec(memory_space=pltpu.VMEM) for _ in outs],
            out_shape=shapes,
            scratch_shapes=list(scratch),
            compiler_params=pltpu.CompilerParams(vmem_limit_bytes=VMEM_LIMIT),
        )(*args)

    return run


def permute(value, partner):
    nx, ny = lax.axis_size("gx"), lax.axis_size("gy")
    pairs = []
    for x in range(nx):
        for y in range(ny):
            u, v = partner(x, y)
            pairs.append((x * ny + y, u * ny + v))
    return lax.ppermute(value, ("gx", "gy"), pairs)


def exchange_x(value):
    nx, ny = lax.axis_size("gx"), lax.axis_size("gy")

    def partner(x, y, near):
        if near:
            return x ^ 1, y
        if 0 < x < nx - 1:
            return ((x + 1) ^ 1) - 1, y
        return (x, y ^ 2) if ny % 4 == 0 else (x, y)

    first = permute(value, lambda x, y: partner(x, y, y % 2 == 0))
    second = permute(value, lambda x, y: partner(x, y, y % 2 == 1))
    return first, second


def exchange_y(near, far):
    ny = lax.axis_size("gy")

    def partner(x, y):
        if 0 < y < ny - 1:
            return x, ((y + 1) ^ 1) - 1
        return x ^ 1, y

    far = permute(far, partner)
    near = permute(near, lambda x, y: (x, y ^ 1))
    return near, far


def swap(value, axis):
    n = lax.axis_size(axis)
    return lax.ppermute(value, axis, [(i, (i + n // 2) % n) for i in range(n)])


def per_device(enthalpy, porosity, active, move_count, move_slot):
    rows, cols, depth = enthalpy.shape
    tx, ty = rows // 2, cols // 2
    count = move_count.reshape(2)
    slots = move_slot.reshape(2, move_slot.shape[-1])
    ranks = slots.shape[1]
    f32, bf16, i16 = jnp.float32, jnp.bfloat16, jnp.int16

    block = ((rows, cols, depth), f32)
    masks = ((mask_at(ranks)[3], SUB, LANES), f32)
    own, enthalpy, porosity, masks = call(
        pack_x, "sssvv", [((2 * rows + 1, cols, depth), bf16), block, block, masks]
    )(active, count, slots, enthalpy, porosity)
    x_near, x_far = exchange_x(own)
    side = ((4 * rows + 1, DEEP, depth), bf16)
    near, far = call(pack_y, "VVV", [side, side])(own, x_near, x_far)
    y_near, y_far = exchange_y(near, far)
    total = rows + 2 * DEEP
    n = total // SUB
    tiles = ((4, tx, ty, depth), f32)
    parcel = ((ranks, 2, tx, ty, depth), i16)
    column = (n, SUB, depth)
    whole = ((cols, *column), f32)
    save = ((EARLY, 2, *column), f32)
    edge = ((DEEP + 1, *column), f32)
    kept = ((PAIRS, *column), f32)
    mid = ((rows, cols - 2 * DEEP, depth), f32)
    strip = ((rows, DEEP, depth), f32)
    state = call(
        inner, "VVVVV", [whole, whole, save, save, ((2, *column), f32)],
        [pltpu.VMEM((2, total * cols, depth), f32)],
    )(own, enthalpy, porosity, x_near, x_far)
    scratch = [
        pltpu.VMEM((2, total * DEEP, depth), f32),
        pltpu.VMEM((2, rows * DEEP, depth), f32),
    ]
    heat_near, pore_near, heat_mid, pore_mid, *ends = call(
        middle, "V" * 6, [strip, strip, mid, mid, edge, edge, kept, kept],
        scratch
        + [
            pltpu.VMEM((2, total * (cols - 2 * DEEP), depth), f32),
            pltpu.VMEM((2, rows * (cols - 2 * DEEP), depth), f32),
        ],
    )(*state, y_near)
    last, first = call(
        far_edge, "V" * 11, [((2, rows, cols, depth), f32), parcel], scratch
    )(masks, *ends, heat_mid, pore_mid, state[4], y_far, heat_near, pore_near)
    heat, pore, later = call(split, "VV", [tiles, tiles, parcel])(masks, last)
    first = swap(first, "gx")
    (second,) = call(resend, "VVV", [parcel])(masks, first, later)
    second = swap(second, "gy")
    heat, pore = call(place, "VVVVV", [tiles, tiles], out_space=None)(
        masks, heat, pore, first, second
    )
    return heat[None, None], pore[None, None]


def solution(mesh):
    placed = (
        P("gx", "gy", None),
        P("gx", "gy", None),
        P("gx", "gy"),
        P("gx", "gy", None),
        P("gx", "gy", None, None),
    )
    out = P("gx", "gy", None, None, None, None)

    return jax.shard_map(
        per_device, mesh=mesh, in_specs=placed, out_specs=(out, out), check_vma=False
    )
```

profile of v0, /device:TPU:0, one launch (start us, length us, event | category | flops | bytes accessed | tf_op | source)
XLA Modules:
  0.0 27.9 jit_solution(15300475388728396731)
XLA Ops:
  0.6 1.0 %shard_map.68 = (bf16[17,32,128]{2,1,0:T(8,128)(2,1)S(1)}, f32[8,32,128]{2,1,0:T(8,128)S(1)}, f32[8,32,128]{2,1,0:T(8,128)S(1)}, f32[36,8,128]{2,1,0:T(8,128)S(1)}) custom-call(s32[2,2]{1,0:T(2,128)} %active_ref.1, s32[2]{0:T(128)} %bitcast.5, s32[2,2]{1,0:T(2,128)} %bitcast.4, f32[8,32,128]{2,1,0:T(8,128)} %heat_ref.1, f32[8,32,128]{2,1,0:T(8,128)} %pore_ref.1), custom_call_target="tpu_custom_call" | custom-call | tf_op jit(solution)/shard_map/pallas_call | solution.py:554
  1.7 3.1 %collective-permute-start = (bf16[17,32,128]{2,1,0:T(8,128)(2,1)S(1)}, bf16[17,32,128]{2,1,0:T(8,128)(2,1)S(1)}, u32[]{:S(2)}, u32[]{:S(2)}) collective-permute-start(bf16[17,32,128]{2,1,0:T(8,128)(2,1)S(1)} %get-tuple-element.29.own_ref), channel_id=1, source_target_pairs={{0,8},{1,3},{2,10},{3,1},{4,12},{5,7},{6,14},{7,5},{8,0},{9,17},{1... | collective-permute-start | bytes 417800 | tf_op jit(solution)/shard_map/ppermute | solution.py:573
  4.8 1.5 %collective-permute-start.1 = (bf16[17,32,128]{2,1,0:T(8,128)(2,1)S(1)}, bf16[17,32,128]{2,1,0:T(8,128)(2,1)S(1)}, u32[]{:S(2)}, u32[]{:S(2)}) collective-permute-start(bf16[17,32,128]{2,1,0:T(8,128)(2,1)S(1)} %get-tuple-element.29.own_ref), channel_id=1, source_target_pairs={{0,2},{1,9},{2,0},{3,11},{4,6},{5,13},{6,4},{7,15},{8,16},{9,1},{1... | collective-permute-start | bytes 417800 | tf_op jit(solution)/shard_map/ppermute | solution.py:573
  6.3 2.5 %collective-permute-done.xa_ref.first_ref = bf16[17,32,128]{2,1,0:T(8,128)(2,1)S(1)} collective-permute-done((bf16[17,32,128]{2,1,0:T(8,128)(2,1)S(1)}, bf16[17,32,128]{2,1,0:T(8,128)(2,1)S(1)}, u32[]{:S(2)}, u32[]{:S(2)}) %collective-permute-start) | collective-permute-done | bytes 139296 | tf_op jit(solution)/shard_map/ppermute | solution.py:573
  8.8 1.0 %collective-permute-done.1.xb_ref.second_ref = bf16[17,32,128]{2,1,0:T(8,128)(2,1)S(1)} collective-permute-done((bf16[17,32,128]{2,1,0:T(8,128)(2,1)S(1)}, bf16[17,32,128]{2,1,0:T(8,128)(2,1)S(1)}, u32[]{:S(2)}, u32[]{:S(2)}) %collective-permute-start.1) | collective-permute-done | bytes 139296 | tf_op jit(solution)/shard_map/ppermute | solution.py:573
  9.8 0.1 shard_map.70
  9.9 0.1 collective-permute-start.2
  10.0 1.4 %collective-permute-start.3 = (bf16[33,8,128]{2,1,0:T(8,128)(2,1)S(1)}, bf16[33,8,128]{2,1,0:T(8,128)(2,1)S(1)}, u32[]{:S(2)}, u32[]{:S(2)}) collective-permute-start(bf16[33,8,128]{2,1,0:T(8,128)(2,1)S(1)} %get-tuple-element.44), channel_id=1, source_target_pairs={{0,8},{1,2},{2,1},{3,4},{4,3},{5,6},{6,5},{7,15},{8,0},{9,10},{10,... | collective-permute-start | bytes 202760 | tf_op jit(solution)/shard_map/ppermute | solution.py:573
  11.4 1.6 %shard_map.69 = (f32[32,3,8,128]{3,2,1,0:T(8,128)S(1)}, f32[32,3,8,128]{3,2,1,0:T(8,128)S(1)}, f32[2,2,3,8,128]{4,3,2,1,0:T(8,128)S(1)}, f32[2,2,3,8,128]{4,3,2,1,0:T(8,128)S(1)}, f32[2,3,8,128]{3,2,1,0:T(8,128)S(1)}) custom-call(bf16[17,32,128]{2,1,0:T(8,128)(2,1)S(1)} %get-tuple-element.29.own_ref, f32[8,32,128]{2,1,0:T(8,128)S(1)} %get-tuple-element.30.heat_ref, ...), custom_call_target="tpu_custom_call" | custom-call | tf_op jit(solution)/shard_map/pallas_call | solution.py:554
  13.0 0.0 collective-permute-done.2.got_ref
  13.0 2.0 %shard_map.71 = (f32[8,8,128]{2,1,0:T(8,128)S(1)}, f32[8,8,128]{2,1,0:T(8,128)S(1)}, f32[8,16,128]{2,1,0:T(8,128)S(1)}, f32[8,16,128]{2,1,0:T(8,128)S(1)}, f32[9...) custom-call(f32[32,3,8,128]{3,2,1,0:T(8,128)S(1)} %get-tuple-element, ...), custom_call_target="tpu_custom_call" | custom-call | tf_op jit(solution)/shard_map/pallas_call | solution.py:554
  15.0 0.0 collective-permute-done.3.got_ref
  15.0 1.1 %shard_map.72 = (f32[2,8,32,128]{3,2,1,0:T(8,128)S(1)}, s16[2,2,4,16,128]{4,3,2,1,0:T(8,128)(2,1)S(1)}) custom-call(f32[36,8,128]{2,1,0:T(8,128)S(1)} %get-tuple-element.28.mask_ref, f32[9,3,8,128]{3,2,1,0:T(8,128)S(1)} %get-tuple-element.38.heat_edge, f32[9,3,8,128]{3,2,1,0:T(8,128)S(1)} %get-tuple-element.39.pore_edge, ...), custom_call_target="tpu_custom_call" | custom-call | tf_op jit(solution)/shard_map/pallas_call | solution.py:554
  16.1 2.7 %collective-permute-start.4 = (s16[2,2,4,16,128]{4,3,2,1,0:T(8,128)(2,1)S(1)}, s16[2,2,4,16,128]{4,3,2,1,0:T(8,128)(2,1)S(1)}, u32[]{:S(2)}, u32[]{:S(2)}) collective-permute-start(s16[2,2,4,16,128]{4,3,2,1,0:T(8,128)(2,1)S(1)} %get-tuple-element.50), channel_id=1, source_target_pairs={{0,16},{8,24},{16,0},{24,8},{1,17},{9,25},{17,1},{25,9},{2,18},{10... | collective-permute-start | bytes 196616 | tf_op jit(solution)/shard_map/ppermute | solution.py:606
  18.9 0.1 shard_map.73
  19.0 3.8 %collective-permute-done.4.got_ref.first_ref = s16[2,2,4,16,128]{4,3,2,1,0:T(8,128)(2,1)S(1)} collective-permute-done((s16[2,2,4,16,128]{4,3,2,1,0:T(8,128)(2,1)S(1)}, s16[2,2,4,16,128]{4,3,2,1,0:T(8,128)(2,1)S(1)}, u32[]{:S(2)}, u32[]{:S(2)}) %collective-permute-start.4) | collective-permute-done | bytes 65568 | tf_op jit(solution)/shard_map/ppermute | solution.py:606
  22.8 1.7 %collective-permute-start.5 = (s16[2,2,4,16,128]{4,3,2,1,0:T(8,128)(2,1)S(1)}, s16[2,2,4,16,128]{4,3,2,1,0:T(8,128)(2,1)S(1)}, u32[]{:S(2)}, u32[]{:S(2)}) collective-permute-start(s16[2,2,4,16,128]{4,3,2,1,0:T(8,128)(2,1)S(1)} %shard_map.74), channel_id=1, source_target_pairs={{0,4},{1,5},{2,6},{3,7},{4,0},{5,1},{6,2},{7,3},{8,12},{9,13},{10,... | collective-permute-start | bytes 196616 | tf_op jit(solution)/shard_map/ppermute | solution.py:606
  24.5 2.7 %collective-permute-done.5.second_ref = s16[2,2,4,16,128]{4,3,2,1,0:T(8,128)(2,1)S(1)} collective-permute-done((s16[2,2,4,16,128]{4,3,2,1,0:T(8,128)(2,1)S(1)}, s16[2,2,4,16,128]{4,3,2,1,0:T(8,128)(2,1)S(1)}, u32[]{:S(2)}, u32[]{:S(2)}) %collective-permute-start.5) | collective-permute-done | bytes 65568 | tf_op jit(solution)/shard_map/ppermute | solution.py:606
  27.1 0.7 %shard_map.75 = (f32[4,4,16,128]{3,2,1,0:T(8,128)}, f32[4,4,16,128]{3,2,1,0:T(8,128)}) custom-call(f32[36,8,128]{2,1,0:T(8,128)S(1)} %get-tuple-element.28.mask_ref, f32[4,4,16,128]{3,2,1,0:T(8,128)S(1)} %get-tuple-element.48.heat_ref, f32[4,4,16,128]{3,2,1,0:T(8,128)S(1)} %get-tuple-element.49.pore_ref, ...), custom_call_target="tpu_custom_call" | custom-call | tf_op jit(solution)/shard_map/pallas_call | solution.py:554
  (1 shorter events, 0.0 us)
Async XLA Ops:
  1.7 7.1 %collective-permute-start = (bf16[17,32,128]{2,1,0:T(8,128)(2,1)S(1)}, bf16[17,32,128]{2,1,0:T(8,128)(2,1)S(1)}, u32[]{:S(2)}, u32[]{:S(2)}) collective-permute-start(bf16[17,32,128]{2,1,0:T(8,128)(2,1)S(1)} %get-tuple-element.29.own_ref), channel_id=1, source_target_pairs={{0,8},{1,3},{2,10},{3,1},{4,12},{5,7},{6,14},{7,5},{8,0},{9,17},{1... | collective-permute-start | bytes 417800 | tf_op jit(solution)/shard_map/ppermute | solution.py:573
  4.8 5.1 %collective-permute-start.1 = (bf16[17,32,128]{2,1,0:T(8,128)(2,1)S(1)}, bf16[17,32,128]{2,1,0:T(8,128)(2,1)S(1)}, u32[]{:S(2)}, u32[]{:S(2)}) collective-permute-start(bf16[17,32,128]{2,1,0:T(8,128)(2,1)S(1)} %get-tuple-element.29.own_ref), channel_id=1, source_target_pairs={{0,2},{1,9},{2,0},{3,11},{4,6},{5,13},{6,4},{7,15},{8,16},{9,1},{1... | collective-permute-start | bytes 417800 | tf_op jit(solution)/shard_map/ppermute | solution.py:573
  9.9 3.1 %collective-permute-start.2 = (bf16[33,8,128]{2,1,0:T(8,128)(2,1)S(1)}, bf16[33,8,128]{2,1,0:T(8,128)(2,1)S(1)}, u32[]{:S(2)}, u32[]{:S(2)}) collective-permute-start(bf16[33,8,128]{2,1,0:T(8,128)(2,1)S(1)} %get-tuple-element.37), channel_id=1, source_target_pairs={{0,1},{1,0},{2,3},{3,2},{4,5},{5,4},{6,7},{7,6},{8,9},{9,8},{10,11... | collective-permute-start | bytes 202760 | tf_op jit(solution)/shard_map/ppermute | solution.py:573
  10.0 5.0 %collective-permute-start.3 = (bf16[33,8,128]{2,1,0:T(8,128)(2,1)S(1)}, bf16[33,8,128]{2,1,0:T(8,128)(2,1)S(1)}, u32[]{:S(2)}, u32[]{:S(2)}) collective-permute-start(bf16[33,8,128]{2,1,0:T(8,128)(2,1)S(1)} %get-tuple-element.44), channel_id=1, source_target_pairs={{0,8},{1,2},{2,1},{3,4},{4,3},{5,6},{6,5},{7,15},{8,0},{9,10},{10,... | collective-permute-start | bytes 202760 | tf_op jit(solution)/shard_map/ppermute | solution.py:573
  16.1 6.6 %collective-permute-start.4 = (s16[2,2,4,16,128]{4,3,2,1,0:T(8,128)(2,1)S(1)}, s16[2,2,4,16,128]{4,3,2,1,0:T(8,128)(2,1)S(1)}, u32[]{:S(2)}, u32[]{:S(2)}) collective-permute-start(s16[2,2,4,16,128]{4,3,2,1,0:T(8,128)(2,1)S(1)} %get-tuple-element.50), channel_id=1, source_target_pairs={{0,16},{8,24},{16,0},{24,8},{1,17},{9,25},{17,1},{25,9},{2,18},{10... | collective-permute-start | bytes 196616 | tf_op jit(solution)/shard_map/ppermute | solution.py:606
  22.8 4.3 %collective-permute-start.5 = (s16[2,2,4,16,128]{4,3,2,1,0:T(8,128)(2,1)S(1)}, s16[2,2,4,16,128]{4,3,2,1,0:T(8,128)(2,1)S(1)}, u32[]{:S(2)}, u32[]{:S(2)}) collective-permute-start(s16[2,2,4,16,128]{4,3,2,1,0:T(8,128)(2,1)S(1)} %shard_map.74), channel_id=1, source_target_pairs={{0,4},{1,5},{2,6},{3,7},{4,0},{5,1},{6,2},{7,3},{8,12},{9,13},{10,... | collective-permute-start | bytes 196616 | tf_op jit(solution)/shard_map/ppermute | solution.py:606
where the time goes:
time: 28 us; the launch traced here: 27.9 us
  starting transfers between devices  10.5 us (38%)
  waiting for transfers between devices  10.1 us (36%)
  Pallas kernels  6.62 us (24%)
  between operations  0.69 us (2%)
    pallas_call x8, Pallas kernels, run(): pl.pallas_call(body, in_specs=[pl.BlockSpec(memory_space=space[c]) for c...  6.62 us
    ppermute x2, waiting for transfers between devices, swap(): return lax.ppermute(value, axis, [(i, (i + n // 2) % n) for i in range(n)])  6.49 us
    ppermute x4, starting transfers between devices, permute(): return lax.ppermute(value, ('gx', 'gy'), pairs)  6.11 us
    ppermute x2, starting transfers between devices, swap(): return lax.ppermute(value, axis, [(i, (i + n // 2) % n) for i in range(n)])  4.4 us
    ppermute x4, waiting for transfers between devices, permute(): return lax.ppermute(value, ('gx', 'gy'), pairs)  3.57 us
  transfers between devices with their start and end apart: 6, of which 4 were waited for; matrix products, arithmetic and copies ran while one was open for 0% of the time, Pallas kernels for 13%

commit v1 on v0

--- a/solution.py
+++ b/solution.py
@@ -13,15 +13,14 @@
 LANES = 128
 VMEM_LIMIT = 16 * 2**20
 
-HEAT_SCALE = 16000.0
-HEAT_SHIFT = 20000.0
-PORE_SCALE = 25000.0
-PORE_SHIFT = 7750.0
+HEAT_SCALE = 25000.0
+HEAT_SHIFT = 32000.0
+PORE_SCALE = 40000.0
+PORE_SHIFT = 7000.0
 
 
 def encode(values, scale, shift):
-    codes = jnp.floor(values * scale + (0.5 - shift))
-    return jnp.clip(codes, -32768.0, 32767.0).astype(jnp.int32).astype(jnp.int16)
+    return jnp.floor(values * scale + (0.5 - shift)).astype(jnp.int32).astype(jnp.int16)
 
 
 def decode(codes, scale, shift):
@@ -418,7 +417,7 @@
                 then = dict(hw)
                 then[c + 1] = kept[0][p]
                 part = (False, then, qw, lo, lo + DEEP, mask_w)
-            new, ours = advance(part, end)
+            new, ours = advance(part, end, twice=step < 2 * PAIRS - 2)
             (qw if pore else hw).update(new)
             waiting.append(ours)
             if step % 2 == 1:

time: 28 us -> 28 us (level)
  no operation moved by 1% of the time
where the time goes in v1:
time: 28 us; the launch traced here: 27.9 us
  starting transfers between devices  10.5 us (38%)
  waiting for transfers between devices  10.1 us (36%)
  Pallas kernels  6.63 us (24%)
  between operations  0.69 us (2%)
    pallas_call x8, Pallas kernels, run(): pl.pallas_call(body, in_specs=[pl.BlockSpec(memory_space=space[c]) for c...  6.63 us
    ppermute x2, waiting for transfers between devices, swap(): return lax.ppermute(value, axis, [(i, (i + n // 2) % n) for i in range(n)])  6.5 us
    ppermute x4, starting transfers between devices, permute(): return lax.ppermute(value, ('gx', 'gy'), pairs)  6.11 us
    ppermute x2, starting transfers between devices, swap(): return lax.ppermute(value, axis, [(i, (i + n // 2) % n) for i in range(n)])  4.4 us
    ppermute x4, waiting for transfers between devices, permute(): return lax.ppermute(value, ('gx', 'gy'), pairs)  3.57 us
  transfers between devices with their start and end apart: 6, of which 4 were waited for; matrix products, arithmetic and copies ran while one was open for 0% of the time, Pallas kernels for 13%

profile of v1, /device:TPU:0, one launch (start us, length us, event | category | flops | bytes accessed | tf_op | source)
XLA Modules:
  0.0 27.9 jit_solution(12395255986823387497)
XLA Ops:
  0.6 1.0 %shard_map.68 = (bf16[17,32,128]{2,1,0:T(8,128)(2,1)S(1)}, f32[8,32,128]{2,1,0:T(8,128)S(1)}, f32[8,32,128]{2,1,0:T(8,128)S(1)}, f32[36,8,128]{2,1,0:T(8,128)S(1)}) custom-call(s32[2,2]{1,0:T(2,128)} %active_ref.1, s32[2]{0:T(128)} %bitcast.5, s32[2,2]{1,0:T(2,128)} %bitcast.4, f32[8,32,128]{2,1,0:T(8,128)} %heat_ref.1, f32[8,32,128]{2,1,0:T(8,128)} %pore_ref.1), custom_call_target="tpu_custom_call" | custom-call | tf_op jit(solution)/shard_map/pallas_call | solution.py:553
  1.7 3.1 %collective-permute-start = (bf16[17,32,128]{2,1,0:T(8,128)(2,1)S(1)}, bf16[17,32,128]{2,1,0:T(8,128)(2,1)S(1)}, u32[]{:S(2)}, u32[]{:S(2)}) collective-permute-start(bf16[17,32,128]{2,1,0:T(8,128)(2,1)S(1)} %get-tuple-element.29.own_ref), channel_id=1, source_target_pairs={{0,8},{1,3},{2,10},{3,1},{4,12},{5,7},{6,14},{7,5},{8,0},{9,17},{1... | collective-permute-start | bytes 417800 | tf_op jit(solution)/shard_map/ppermute | solution.py:572
  4.8 1.5 %collective-permute-start.1 = (bf16[17,32,128]{2,1,0:T(8,128)(2,1)S(1)}, bf16[17,32,128]{2,1,0:T(8,128)(2,1)S(1)}, u32[]{:S(2)}, u32[]{:S(2)}) collective-permute-start(bf16[17,32,128]{2,1,0:T(8,128)(2,1)S(1)} %get-tuple-element.29.own_ref), channel_id=1, source_target_pairs={{0,2},{1,9},{2,0},{3,11},{4,6},{5,13},{6,4},{7,15},{8,16},{9,1},{1... | collective-permute-start | bytes 417800 | tf_op jit(solution)/shard_map/ppermute | solution.py:572
  6.3 2.5 %collective-permute-done.xa_ref.first_ref = bf16[17,32,128]{2,1,0:T(8,128)(2,1)S(1)} collective-permute-done((bf16[17,32,128]{2,1,0:T(8,128)(2,1)S(1)}, bf16[17,32,128]{2,1,0:T(8,128)(2,1)S(1)}, u32[]{:S(2)}, u32[]{:S(2)}) %collective-permute-start) | collective-permute-done | bytes 139296 | tf_op jit(solution)/shard_map/ppermute | solution.py:572
  8.8 1.0 %collective-permute-done.1.xb_ref.second_ref = bf16[17,32,128]{2,1,0:T(8,128)(2,1)S(1)} collective-permute-done((bf16[17,32,128]{2,1,0:T(8,128)(2,1)S(1)}, bf16[17,32,128]{2,1,0:T(8,128)(2,1)S(1)}, u32[]{:S(2)}, u32[]{:S(2)}) %collective-permute-start.1) | collective-permute-done | bytes 139296 | tf_op jit(solution)/shard_map/ppermute | solution.py:572
  9.8 0.1 shard_map.70
  9.9 0.1 collective-permute-start.2
  10.0 1.4 %collective-permute-start.3 = (bf16[33,8,128]{2,1,0:T(8,128)(2,1)S(1)}, bf16[33,8,128]{2,1,0:T(8,128)(2,1)S(1)}, u32[]{:S(2)}, u32[]{:S(2)}) collective-permute-start(bf16[33,8,128]{2,1,0:T(8,128)(2,1)S(1)} %get-tuple-element.44), channel_id=1, source_target_pairs={{0,8},{1,2},{2,1},{3,4},{4,3},{5,6},{6,5},{7,15},{8,0},{9,10},{10,... | collective-permute-start | bytes 202760 | tf_op jit(solution)/shard_map/ppermute | solution.py:572
  11.4 1.6 %shard_map.69 = (f32[32,3,8,128]{3,2,1,0:T(8,128)S(1)}, f32[32,3,8,128]{3,2,1,0:T(8,128)S(1)}, f32[2,2,3,8,128]{4,3,2,1,0:T(8,128)S(1)}, f32[2,2,3,8,128]{4,3,2,1,0:T(8,128)S(1)}, f32[2,3,8,128]{3,2,1,0:T(8,128)S(1)}) custom-call(bf16[17,32,128]{2,1,0:T(8,128)(2,1)S(1)} %get-tuple-element.29.own_ref, f32[8,32,128]{2,1,0:T(8,128)S(1)} %get-tuple-element.30.heat_ref, ...), custom_call_target="tpu_custom_call" | custom-call | tf_op jit(solution)/shard_map/pallas_call | solution.py:553
  13.0 0.0 collective-permute-done.2.got_ref
  13.0 2.1 %shard_map.71 = (f32[8,8,128]{2,1,0:T(8,128)S(1)}, f32[8,8,128]{2,1,0:T(8,128)S(1)}, f32[8,16,128]{2,1,0:T(8,128)S(1)}, f32[8,16,128]{2,1,0:T(8,128)S(1)}, f32[9...) custom-call(f32[32,3,8,128]{3,2,1,0:T(8,128)S(1)} %get-tuple-element, ...), custom_call_target="tpu_custom_call" | custom-call | tf_op jit(solution)/shard_map/pallas_call | solution.py:553
  15.1 0.0 collective-permute-done.3.got_ref
  15.1 1.1 %shard_map.72 = (f32[2,8,32,128]{3,2,1,0:T(8,128)S(1)}, s16[2,2,4,16,128]{4,3,2,1,0:T(8,128)(2,1)S(1)}) custom-call(f32[36,8,128]{2,1,0:T(8,128)S(1)} %get-tuple-element.28.mask_ref, f32[9,3,8,128]{3,2,1,0:T(8,128)S(1)} %get-tuple-element.38.heat_edge, f32[9,3,8,128]{3,2,1,0:T(8,128)S(1)} %get-tuple-element.39.pore_edge, ...), custom_call_target="tpu_custom_call" | custom-call | tf_op jit(solution)/shard_map/pallas_call | solution.py:553
  16.2 2.7 %collective-permute-start.4 = (s16[2,2,4,16,128]{4,3,2,1,0:T(8,128)(2,1)S(1)}, s16[2,2,4,16,128]{4,3,2,1,0:T(8,128)(2,1)S(1)}, u32[]{:S(2)}, u32[]{:S(2)}) collective-permute-start(s16[2,2,4,16,128]{4,3,2,1,0:T(8,128)(2,1)S(1)} %get-tuple-element.50), channel_id=1, source_target_pairs={{0,16},{8,24},{16,0},{24,8},{1,17},{9,25},{17,1},{25,9},{2,18},{10... | collective-permute-start | bytes 196616 | tf_op jit(solution)/shard_map/ppermute | solution.py:605
  18.9 0.1 shard_map.73
  19.0 3.8 %collective-permute-done.4.got_ref.first_ref = s16[2,2,4,16,128]{4,3,2,1,0:T(8,128)(2,1)S(1)} collective-permute-done((s16[2,2,4,16,128]{4,3,2,1,0:T(8,128)(2,1)S(1)}, s16[2,2,4,16,128]{4,3,2,1,0:T(8,128)(2,1)S(1)}, u32[]{:S(2)}, u32[]{:S(2)}) %collective-permute-start.4) | collective-permute-done | bytes 65568 | tf_op jit(solution)/shard_map/ppermute | solution.py:605
  22.8 1.7 %collective-permute-start.5 = (s16[2,2,4,16,128]{4,3,2,1,0:T(8,128)(2,1)S(1)}, s16[2,2,4,16,128]{4,3,2,1,0:T(8,128)(2,1)S(1)}, u32[]{:S(2)}, u32[]{:S(2)}) collective-permute-start(s16[2,2,4,16,128]{4,3,2,1,0:T(8,128)(2,1)S(1)} %shard_map.74), channel_id=1, source_target_pairs={{0,4},{1,5},{2,6},{3,7},{4,0},{5,1},{6,2},{7,3},{8,12},{9,13},{10,... | collective-permute-start | bytes 196616 | tf_op jit(solution)/shard_map/ppermute | solution.py:605
  24.5 2.7 %collective-permute-done.5.second_ref = s16[2,2,4,16,128]{4,3,2,1,0:T(8,128)(2,1)S(1)} collective-permute-done((s16[2,2,4,16,128]{4,3,2,1,0:T(8,128)(2,1)S(1)}, s16[2,2,4,16,128]{4,3,2,1,0:T(8,128)(2,1)S(1)}, u32[]{:S(2)}, u32[]{:S(2)}) %collective-permute-start.5) | collective-permute-done | bytes 65568 | tf_op jit(solution)/shard_map/ppermute | solution.py:605
  27.2 0.7 %shard_map.75 = (f32[4,4,16,128]{3,2,1,0:T(8,128)}, f32[4,4,16,128]{3,2,1,0:T(8,128)}) custom-call(f32[36,8,128]{2,1,0:T(8,128)S(1)} %get-tuple-element.28.mask_ref, f32[4,4,16,128]{3,2,1,0:T(8,128)S(1)} %get-tuple-element.48.heat_ref, f32[4,4,16,128]{3,2,1,0:T(8,128)S(1)} %get-tuple-element.49.pore_ref, ...), custom_call_target="tpu_custom_call" | custom-call | tf_op jit(solution)/shard_map/pallas_call | solution.py:553
  (1 shorter events, 0.0 us)
Async XLA Ops:
  1.7 7.1 %collective-permute-start = (bf16[17,32,128]{2,1,0:T(8,128)(2,1)S(1)}, bf16[17,32,128]{2,1,0:T(8,128)(2,1)S(1)}, u32[]{:S(2)}, u32[]{:S(2)}) collective-permute-start(bf16[17,32,128]{2,1,0:T(8,128)(2,1)S(1)} %get-tuple-element.29.own_ref), channel_id=1, source_target_pairs={{0,8},{1,3},{2,10},{3,1},{4,12},{5,7},{6,14},{7,5},{8,0},{9,17},{1... | collective-permute-start | bytes 417800 | tf_op jit(solution)/shard_map/ppermute | solution.py:572
  4.8 5.1 %collective-permute-start.1 = (bf16[17,32,128]{2,1,0:T(8,128)(2,1)S(1)}, bf16[17,32,128]{2,1,0:T(8,128)(2,1)S(1)}, u32[]{:S(2)}, u32[]{:S(2)}) collective-permute-start(bf16[17,32,128]{2,1,0:T(8,128)(2,1)S(1)} %get-tuple-element.29.own_ref), channel_id=1, source_target_pairs={{0,2},{1,9},{2,0},{3,11},{4,6},{5,13},{6,4},{7,15},{8,16},{9,1},{1... | collective-permute-start | bytes 417800 | tf_op jit(solution)/shard_map/ppermute | solution.py:572
  9.9 3.1 %collective-permute-start.2 = (bf16[33,8,128]{2,1,0:T(8,128)(2,1)S(1)}, bf16[33,8,128]{2,1,0:T(8,128)(2,1)S(1)}, u32[]{:S(2)}, u32[]{:S(2)}) collective-permute-start(bf16[33,8,128]{2,1,0:T(8,128)(2,1)S(1)} %get-tuple-element.37), channel_id=1, source_target_pairs={{0,1},{1,0},{2,3},{3,2},{4,5},{5,4},{6,7},{7,6},{8,9},{9,8},{10,11... | collective-permute-start | bytes 202760 | tf_op jit(solution)/shard_map/ppermute | solution.py:572
  10.0 5.1 %collective-permute-start.3 = (bf16[33,8,128]{2,1,0:T(8,128)(2,1)S(1)}, bf16[33,8,128]{2,1,0:T(8,128)(2,1)S(1)}, u32[]{:S(2)}, u32[]{:S(2)}) collective-permute-start(bf16[33,8,128]{2,1,0:T(8,128)(2,1)S(1)} %get-tuple-element.44), channel_id=1, source_target_pairs={{0,8},{1,2},{2,1},{3,4},{4,3},{5,6},{6,5},{7,15},{8,0},{9,10},{10,... | collective-permute-start | bytes 202760 | tf_op jit(solution)/shard_map/ppermute | solution.py:572
  16.2 6.6 %collective-permute-start.4 = (s16[2,2,4,16,128]{4,3,2,1,0:T(8,128)(2,1)S(1)}, s16[2,2,4,16,128]{4,3,2,1,0:T(8,128)(2,1)S(1)}, u32[]{:S(2)}, u32[]{:S(2)}) collective-permute-start(s16[2,2,4,16,128]{4,3,2,1,0:T(8,128)(2,1)S(1)} %get-tuple-element.50), channel_id=1, source_target_pairs={{0,16},{8,24},{16,0},{24,8},{1,17},{9,25},{17,1},{25,9},{2,18},{10... | collective-permute-start | bytes 196616 | tf_op jit(solution)/shard_map/ppermute | solution.py:605
  22.8 4.3 %collective-permute-start.5 = (s16[2,2,4,16,128]{4,3,2,1,0:T(8,128)(2,1)S(1)}, s16[2,2,4,16,128]{4,3,2,1,0:T(8,128)(2,1)S(1)}, u32[]{:S(2)}, u32[]{:S(2)}) collective-permute-start(s16[2,2,4,16,128]{4,3,2,1,0:T(8,128)(2,1)S(1)} %shard_map.74), channel_id=1, source_target_pairs={{0,4},{1,5},{2,6},{3,7},{4,0},{5,1},{6,2},{7,3},{8,12},{9,13},{10,... | collective-permute-start | bytes 196616 | tf_op jit(solution)/shard_map/ppermute | solution.py:605
